TPU v7x, 32 devices: a whole 2x2x4 slice. The times are simulated.
32 devices in a mesh: dp: 2 (over y), ctx: 4 (over z), fsdp: 4 (over x, core).
Axes of the slice: x: 2, y: 2, z: 4, core: 2. Of those that a mesh axis runs over, the one named last changes fastest.
Arguments:
- layer_input: bfloat16 [8, 2048, 768], P(('dp', 'fsdp'), 'ctx'), may hold values from -6 to 6
- first_values: bfloat16 [8, 2048, 384], P(('dp', 'fsdp'), 'ctx'), may hold values from -6 to 6
- segment_ids: int32 [8, 2048], P(('dp', 'fsdp')), may hold values from 0 to 7, never falling along the last dimension, each value on 1 to 1024 neighbouring positions
- pairing: int32 [8], replicated, may hold values from 0 to 7, as said below
- norm_gains: bfloat16 [2, 768], P(None, 'fsdp'), may hold values from 0.099609375 to 1.8984375
- norm_biases: bfloat16 [2, 768], P(None, 'fsdp'), may hold values from -2 to 2
- w_qkv: bfloat16 [768, 1920], P('fsdp'), may hold values from -0.21875 to 0.21875
- w_out: bfloat16 [768, 768], P('fsdp'), may hold values from -0.875 to 0.875
- w_up: bfloat16 [768, 3072], P(None, 'fsdp'), may hold values from -0.21875 to 0.21875
- w_down: bfloat16 [3072, 768], P('fsdp'), may hold values from -0.109375 to 0.109375
- cotangent: bfloat16 [8, 2048, 768], P(('dp', 'fsdp'), 'ctx'), may hold values from -6 to 6
Outputs:
- layer_out: bfloat16 [8, 2048, 768], P(('dp', 'fsdp'), 'ctx')
- input_grad: float32 [8, 2048, 768], P(('dp', 'fsdp'), 'ctx')
- first_values_grad: float32 [8, 2048, 384], P(('dp', 'fsdp'), 'ctx')
- gains_grad: float32 [2, 768], P(None, 'fsdp')
- biases_grad: float32 [2, 768], P(None, 'fsdp')
- qkv_grad: float32 [768, 1920], P('fsdp')
- out_grad: float32 [768, 768], P('fsdp')
- up_grad: float32 [768, 3072], P(None, 'fsdp')
- down_grad: float32 [3072, 768], P('fsdp')
Inputs may be any that keep to these rules, and one draw needn't show every extreme that they name: `segment_ids`: along each sequence the ids never fall; each document holds 1 to 1024 positions, one exactly that many. `pairing`: every block is named once; entries 2c and 2c + 1 name blocks b and 7 - b for some b, in either order.
All inputs are finite; a program needn't handle non-finite values.
Results may differ from a plain program's by a relative error of at most 0.019.
Values may be sent and summed in bfloat16 or wider, within the bound.
No kernel may reach another device: no remote copies, remote signals or barrier semaphores. Data moves between devices by JAX's collectives and lax.ppermute only.
A program may use at most 192 MiB of HBM per device.

v0:
```python
import jax
import jax.numpy as jnp
from jax import lax
from jax.sharding import PartitionSpec as P

D = 768
HEADS = 12
HD = 64
VH = 6
EPSILON = 1e-05
NEGATIVE = -1e30


def norm_layer(values_in, gain, bias):
    center = jnp.mean(values_in, axis=-1, keepdims=True)
    centred = values_in - center
    spread = jnp.mean(centred * centred, axis=-1, keepdims=True)
    return centred * lax.rsqrt(spread + EPSILON) * gain + bias


def gelu_tanh(values_in):
    return jax.nn.gelu(values_in, approximate=True)


def block_scores(query_part, key_part, query_pos, query_doc, key_pos, key_doc):
    scale = HD ** (-0.5)
    raw = (
        jnp.einsum("rhd,khd->hrk", query_part, key_part, preferred_element_type=jnp.float32) * scale
    )
    allowed = (key_pos[None, :] <= query_pos[:, None]) & (key_doc[None, :] == query_doc[:, None])
    return (raw, allowed[None])


def body(
    layer_input,
    first_values,
    segment_ids,
    pairing,
    norm_gains,
    norm_biases,
    w_qkv,
    w_out,
    w_up,
    w_down,
    cotangent,
):
    scale = HD ** (-0.5)
    ctx_index = lax.axis_index("ctx")
    local_rows = layer_input.shape[1]
    half_rows = local_rows // 2
    seq_length = local_rows * lax.axis_size("ctx")
    key_block = min(512, seq_length)
    key_count = seq_length // key_block
    offsets = jnp.arange(half_rows, dtype=jnp.int32)
    all_pos = (pairing[:, None] * half_rows + offsets[None, :]).reshape(seq_length)
    own_blocks = lax.dynamic_slice_in_dim(pairing, 2 * ctx_index, 2)
    own_pos = (own_blocks[:, None] * half_rows + offsets[None, :]).reshape(local_rows)
    doc_row = segment_ids[0]
    all_doc = jnp.take(doc_row, all_pos)
    own_doc = jnp.take(doc_row, own_pos)
    gathered = (
        lax.all_gather(norm_gains, "fsdp", axis=1, tiled=True),
        lax.all_gather(norm_biases, "fsdp", axis=1, tiled=True),
        lax.all_gather(w_qkv, "fsdp", axis=0, tiled=True),
        lax.all_gather(w_out, "fsdp", axis=0, tiled=True),
        lax.all_gather(w_up, "fsdp", axis=1, tiled=True),
        lax.all_gather(w_down, "fsdp", axis=0, tiled=True),
    )
    gains_all, biases_all, qkv_full, out_full, up_full, down_full = gathered
    gains = gains_all.astype(jnp.float32)
    biases = biases_all.astype(jnp.float32)
    inputs = layer_input[0].astype(jnp.float32)
    normed_one, norm_one_back = jax.vjp(norm_layer, inputs, gains[0], biases[0])
    h_one = normed_one.astype(jnp.bfloat16)
    qkv_low = jnp.dot(h_one, qkv_full, preferred_element_type=jnp.float32).astype(jnp.bfloat16)
    query_low = qkv_low[:, :D]
    key_low = qkv_low[:, D : 2 * D]
    fresh_low = qkv_low[:, 2 * D :]
    values_low = jnp.concatenate([fresh_low, first_values[0]], axis=1)
    keys_all, values_all = (
        lax.all_gather(key_low, "ctx", axis=0, tiled=True),
        lax.all_gather(values_low, "ctx", axis=0, tiled=True),
    )
    query_heads = query_low.reshape(local_rows, HEADS, HD)
    key_blocks = keys_all.reshape(key_count, key_block, HEADS, HD)
    value_blocks = values_all.reshape(key_count, key_block, HEADS, HD)
    pos_blocks = all_pos.reshape(key_count, key_block)
    doc_blocks = all_doc.reshape(key_count, key_block)

    def stats_step(carry, block):
        running_top, running_total = carry
        key_part, key_pos, key_doc = block
        raw, allowed = block_scores(query_heads, key_part, own_pos, own_doc, key_pos, key_doc)
        masked = jnp.where(allowed, raw, NEGATIVE)
        new_top = jnp.maximum(running_top, jnp.max(masked, axis=-1))
        terms = jnp.where(allowed, jnp.exp(raw - new_top[..., None]), 0.0)
        running_total = running_total * jnp.exp(running_top - new_top) + jnp.sum(terms, axis=-1)
        return ((new_top, running_total), None)

    start_top = jnp.full((HEADS, local_rows), NEGATIVE, jnp.float32)
    start_total = jnp.zeros((HEADS, local_rows), jnp.float32)
    (final_top, final_total), _ = lax.scan(
        stats_step, (start_top, start_total), (key_blocks, pos_blocks, doc_blocks)
    )
    log_total = final_top + jnp.log(final_total)

    def mix_step(accum, block):
        key_part, value_part, key_pos, key_doc = block
        raw, allowed = block_scores(query_heads, key_part, own_pos, own_doc, key_pos, key_doc)
        probs = jnp.where(allowed, jnp.exp(raw - log_total[..., None]), 0.0).astype(jnp.bfloat16)
        return (
            accum
            + jnp.einsum("hrk,khd->rhd", probs, value_part, preferred_element_type=jnp.float32),
            None,
        )

    mixed, _ = lax.scan(
        mix_step,
        jnp.zeros((local_rows, HEADS, HD), jnp.float32),
        (key_blocks, value_blocks, pos_blocks, doc_blocks),
    )
    attn_low = mixed.reshape(local_rows, D).astype(jnp.bfloat16)
    resid = inputs + jnp.dot(attn_low, out_full, preferred_element_type=jnp.float32)
    normed_two, norm_two_back = jax.vjp(norm_layer, resid, gains[1], biases[1])
    h_two = normed_two.astype(jnp.bfloat16)
    upper = jnp.dot(h_two, up_full, preferred_element_type=jnp.float32)
    active, gelu_back = jax.vjp(gelu_tanh, upper)
    active_low = active.astype(jnp.bfloat16)
    layer_out = (resid + jnp.dot(active_low, down_full, preferred_element_type=jnp.float32)).astype(
        jnp.bfloat16
    )
    regathered = (
        lax.all_gather(norm_gains, "fsdp", axis=1, tiled=True),
        lax.all_gather(norm_biases, "fsdp", axis=1, tiled=True),
        lax.all_gather(w_qkv, "fsdp", axis=0, tiled=True),
        lax.all_gather(w_out, "fsdp", axis=0, tiled=True),
        lax.all_gather(w_up, "fsdp", axis=1, tiled=True),
        lax.all_gather(w_down, "fsdp", axis=0, tiled=True),
    )
    qkv_back = regathered[2]
    out_back = regathered[3]
    up_back = regathered[4]
    down_back = regathered[5]
    cot_low = cotangent[0]
    cot_full = cot_low.astype(jnp.float32)
    down_grad = jnp.dot(active_low.T, cot_low, preferred_element_type=jnp.float32)
    dactive = jnp.dot(cot_low, down_back.T, preferred_element_type=jnp.float32)
    dupper_low = gelu_back(dactive)[0].astype(jnp.bfloat16)
    up_grad = jnp.dot(h_two.T, dupper_low, preferred_element_type=jnp.float32)
    dh_two = jnp.dot(dupper_low, up_back.T, preferred_element_type=jnp.float32)
    dresid_norm, gain_two_grad, bias_two_grad = norm_two_back(dh_two)
    dresid = cot_full + dresid_norm
    dbranch_low = dresid.astype(jnp.bfloat16)
    out_grad = jnp.dot(attn_low.T, dbranch_low, preferred_element_type=jnp.float32)
    dmixed_low = jnp.dot(dbranch_low, out_back.T, preferred_element_type=jnp.float32).astype(
        jnp.bfloat16
    )
    dmixed_heads = dmixed_low.reshape(local_rows, HEADS, HD)
    row_terms = jnp.sum(dmixed_heads.astype(jnp.float32) * mixed, axis=-1).T

    def grad_step(accum, block):
        key_part, value_part, key_pos, key_doc = block
        raw, allowed = block_scores(query_heads, key_part, own_pos, own_doc, key_pos, key_doc)
        probs = jnp.where(allowed, jnp.exp(raw - log_total[..., None]), 0.0)
        dprobs = jnp.einsum(
            "rhd,khd->hrk", dmixed_heads, value_part, preferred_element_type=jnp.float32
        )
        dscore_low = (probs * (dprobs - row_terms[..., None])).astype(jnp.bfloat16)
        accum = accum + jnp.einsum(
            "hrk,khd->rhd", dscore_low, key_part, preferred_element_type=jnp.float32
        )
        dkey_part = jnp.einsum(
            "hrk,rhd->khd", dscore_low, query_heads, preferred_element_type=jnp.float32
        )
        dvalue_part = jnp.einsum(
            "hrk,rhd->khd",
            probs.astype(jnp.bfloat16),
            dmixed_heads,
            preferred_element_type=jnp.float32,
        )
        return (accum, (dkey_part, dvalue_part))

    dquery_sum, (dkey_parts, dvalue_parts) = lax.scan(
        grad_step,
        jnp.zeros((local_rows, HEADS, HD), jnp.float32),
        (key_blocks, value_blocks, pos_blocks, doc_blocks),
    )
    dkeys_all = dkey_parts.reshape(seq_length, D) * scale
    dvalues_all = dvalue_parts.reshape(seq_length, D)
    own_dkeys, own_dvalues = (
        lax.psum_scatter(
            dkeys_all.astype(jnp.bfloat16), "ctx", scatter_dimension=0, tiled=True
        ).astype(jnp.float32),
        lax.psum_scatter(
            dvalues_all.astype(jnp.bfloat16), "ctx", scatter_dimension=0, tiled=True
        ).astype(jnp.float32),
    )
    dquery = dquery_sum.reshape(local_rows, D) * scale
    fresh_width = VH * HD
    first_grad = own_dvalues[:, fresh_width:]
    dqkv_low = jnp.concatenate(
        [
            dquery.astype(jnp.bfloat16),
            own_dkeys.astype(jnp.bfloat16),
            own_dvalues[:, :fresh_width].astype(jnp.bfloat16),
        ],
        axis=1,
    )
    qkv_grad = jnp.dot(h_one.T, dqkv_low, preferred_element_type=jnp.float32)
    dh_one = jnp.dot(dqkv_low, qkv_back.T, preferred_element_type=jnp.float32)
    dinput_norm, gain_one_grad, bias_one_grad = norm_one_back(dh_one)
    input_grad = dresid + dinput_norm
    gain_grads = jnp.stack([gain_one_grad, gain_two_grad])
    bias_grads = jnp.stack([bias_one_grad, bias_two_grad])
    shares = (
        lax.psum_scatter(
            gain_grads.astype(jnp.bfloat16), "fsdp", scatter_dimension=1, tiled=True
        ).astype(jnp.float32),
        lax.psum_scatter(
            bias_grads.astype(jnp.bfloat16), "fsdp", scatter_dimension=1, tiled=True
        ).astype(jnp.float32),
        lax.psum_scatter(
            qkv_grad.astype(jnp.bfloat16), "fsdp", scatter_dimension=0, tiled=True
        ).astype(jnp.float32),
        lax.psum_scatter(
            out_grad.astype(jnp.bfloat16), "fsdp", scatter_dimension=0, tiled=True
        ).astype(jnp.float32),
        lax.psum_scatter(
            up_grad.astype(jnp.bfloat16), "fsdp", scatter_dimension=1, tiled=True
        ).astype(jnp.float32),
        lax.psum_scatter(
            down_grad.astype(jnp.bfloat16), "fsdp", scatter_dimension=0, tiled=True
        ).astype(jnp.float32),
    )
    summed = (
        lax.psum(shares[0].astype(jnp.bfloat16), ("dp", "ctx")).astype(jnp.float32),
        lax.psum(shares[1].astype(jnp.bfloat16), ("dp", "ctx")).astype(jnp.float32),
        lax.psum(shares[2].astype(jnp.bfloat16), ("dp", "ctx")).astype(jnp.float32),
        lax.psum(shares[3].astype(jnp.bfloat16), ("dp", "ctx")).astype(jnp.float32),
        lax.psum(shares[4].astype(jnp.bfloat16), ("dp", "ctx")).astype(jnp.float32),
        lax.psum(shares[5].astype(jnp.bfloat16), ("dp", "ctx")).astype(jnp.float32),
    )
    return (
        layer_out[None],
        input_grad[None],
        first_grad[None],
        summed[0],
        summed[1],
        summed[2],
        summed[3],
        summed[4],
        summed[5],
    )


def solution(mesh):
    in_specs = (
        P(("dp", "fsdp"), "ctx", None),
        P(("dp", "fsdp"), "ctx", None),
        P(("dp", "fsdp"), None),
        P(),
        P(None, "fsdp"),
        P(None, "fsdp"),
        P("fsdp", None),
        P("fsdp", None),
        P(None, "fsdp"),
        P("fsdp", None),
        P(("dp", "fsdp"), "ctx", None),
    )
    out_specs = (
        P(("dp", "fsdp"), "ctx", None),
        P(("dp", "fsdp"), "ctx", None),
        P(("dp", "fsdp"), "ctx", None),
        P(None, "fsdp"),
        P(None, "fsdp"),
        P("fsdp", None),
        P("fsdp", None),
        P(None, "fsdp"),
        P("fsdp", None),
    )
    return jax.shard_map(body, mesh=mesh, in_specs=in_specs, out_specs=out_specs, check_vma=False)
```

profile of v0, /device:TPU:0, one launch (start us, length us, event | category | flops | bytes accessed | tf_op | source)
XLA Modules:
  0.0 874.5 jit_solution(13623779563315954214)
XLA Ops:
  23.6 16.1 %all-gather.9.cloned.1.call-done = bf16[768,1920]{1,0:T(8,128)(2,1)} async-done(((bf16[192,1920]{1,0:T(8,128)(2,1)}), bf16[768,1920]{1,0:T(8,128)(2,1)}) %all-gather.9.cloned.1.call-update) | async-done | bytes 2949136 | tf_op jit(solution)/shard_map/all_gather | solution.py:64
  51.7 11.8 %gather_fusion = s32[2048]{0:T(1024)S(1)} fusion(s32[2048]{0:T(1024)S(1)} %bitcast.284, s32[2048]{0:T(1024)S(1)} %broadcast_clamp_fusion), kind=kCustom, calls=%fused_computation | custom fusion | bytes 24576 | tf_op jit(solution)/shard_map/jit(_take)/gather | solution.py:59
  65.0 43.7 %all-gather.13.cloned.1.call-done = bf16[2048,768]{1,0:T(8,128)(2,1)} async-done(((bf16[512,768]{1,0:T(8,128)(2,1)}), bf16[2048,768]{1,0:T(8,128)(2,1)}) %all-gather.13.cloned.1.call-update) | async-done | bytes 3145744 | tf_op jit(solution)/shard_map/all_gather | solution.py:81
  123.9 24.9 %while.39 = (s32[]{:T(128)}, f32[12,512]{1,0:T(8,128)S(1)}, f32[12,512]{1,0:T(8,128)S(1)}, s32[4,512]{1,0:T(4,128)S(1)}, s32[4,512]{1,0:T(4,128)S(1)}, /*index=5...) while((s32[]{:T(128)}, f32[12,512]{1,0:T(8,128)S(1)}, ...), condition=%wide.region_5.6_spmd.clone, body=%wide.region_2.5_spmd.clone.sunk | while | flops 425490944 | bytes 27867280 | solution.py:102
  148.8 24.2 %all-gather.11.cloned.1.call-done = bf16[2048,768]{1,0:T(8,128)(2,1)} async-done(((bf16[512,768]{1,0:T(8,128)(2,1)}), bf16[2048,768]{1,0:T(8,128)(2,1)}) %all-gather.11.cloned.1.call-update) | async-done | bytes 3145744 | tf_op jit(solution)/shard_map/all_gather | solution.py:82
  188.3 23.0 %while.40 = (s32[]{:T(128)}, f32[512,12,64]{0,2,1:T(8,128)S(1)}, bf16[4,512,12,64]{1,3,2,0:T(8,128)(2,1)}, s32[4,512]{1,0:T(4,128)S(1)}, s32[4,512]{1,0:T(4,128)...) while((s32[]{:T(128)}, f32[512,12,64]{0,2,1:T(8,128)S(1)}, ...), condition=%wide.region_7.8_spmd.clone, body=%wide.region_6.7_spmd.clone.sunk | while | flops 819462656 | bytes 6078098 | solution.py:117
  216.2 13.3 %all-gather.17.cloned.1.call-done = bf16[768,3072]{1,0:T(8,128)(2,1)} async-done(((bf16[768,768]{1,0:T(8,128)(2,1)}), bf16[768,3072]{1,0:T(8,128)(2,1)}) %all-gather.17.cloned.1.call-update) | async-done | bytes 4718608 | tf_op jit(solution)/shard_map/all_gather | solution.py:66
  229.5 8.2 fusion.88
  237.7 30.7 %all-gather.19.cloned.1.call-done = bf16[3072,768]{1,0:T(8,128)(2,1)} async-done(((bf16[768,768]{1,0:T(8,128)(2,1)}), bf16[3072,768]{1,0:T(8,128)(2,1)}) %all-gather.19.cloned.1.call-update) | async-done | bytes 4718608 | tf_op jit(solution)/shard_map/all_gather | solution.py:67
  268.4 9.3 %fusion.58 = bf16[512,3072]{1,0:T(8,128)(2,1)S(1)} fusion(f32[512,3072]{1,0:T(8,128)} %fusion.88, bf16[3072,768]{1,0:T(8,128)(2,1)} %all-gather.19.cloned.1.call-done, bf16[1,512,768]{2,1,0:T(8,128)(2,1)S(1)} %copy-done.13), kind=kOutput, calls=%fused_computation.72 | convolution fusion | flops 2447376384 | bytes 14942208 | tf_op jit(solution)/shard_map/dot_general | solution.py:147
  287.0 88.2 %while.41 = (s32[]{:T(128)}, f32[512,12,64]{0,2,1:T(8,128)}, f32[4,512,12,64]{1,3,2,0:T(8,128)}, bf16[4,512,12,64]{1,3,2,0:T(8,128)(2,1)}, bf16[4,512,12,64]{1,3...) while((s32[]{:T(128)}, f32[512,12,64]{0,2,1:T(8,128)}, ...), condition=%wide.region_14.15_spmd.clone, body=%wide.region_13.14_spmd.clone.sunk | while | flops 2046296576 | bytes 81885488 | solution.py:183
  394.5 6.5 convolution_convert_fusion.1
  402.1 8.3 convolution_convert_fusion
  412.9 29.8 %reduce-scatter.15.cloned.1.call-done = bf16[512,768]{0,1:T(8,128)(2,1)} async-done(((bf16[2048,768]{0,1:T(8,128)(2,1)}), bf16[512,768]{0,1:T(8,128)(2,1)}) %reduce-scatter.15.cloned.1.call-update) | async-done | bytes 786448 | tf_op jit(solution)/shard_map/reduce_scatter | solution.py:194
  444.9 60.4 %reduce-scatter.13.cloned.1.call-done = bf16[512,768]{0,1:T(8,128)(2,1)} async-done(((bf16[2048,768]{0,1:T(8,128)(2,1)}), bf16[512,768]{0,1:T(8,128)(2,1)}) %reduce-scatter.13.cloned.1.call-update) | async-done | bytes 786448 | tf_op jit(solution)/shard_map/reduce_scatter | solution.py:191
  518.9 15.4 %reduce-scatter.19.cloned.1.call-done = bf16[192,768]{1,0:T(8,128)(2,1)} async-done(((bf16[768,768]{1,0:T(8,128)(2,1)}), bf16[192,768]{1,0:T(8,128)(2,1)}) %reduce-scatter.19.cloned.1.call-update) | async-done | bytes 294928 | tf_op jit(solution)/shard_map/reduce_scatter | solution.py:225
  534.2 50.4 %reduce-scatter.21.cloned.1.call-done = bf16[768,768]{1,0:T(8,128)(2,1)} async-done(((bf16[768,3072]{1,0:T(8,128)(2,1)}), bf16[768,768]{1,0:T(8,128)(2,1)}) %reduce-scatter.21.cloned.1.call-update) | async-done | bytes 1179664 | tf_op jit(solution)/shard_map/reduce_scatter | solution.py:228
  584.7 50.4 %reduce-scatter.23.cloned.1.call-done = bf16[768,768]{1,0:T(8,128)(2,1)} async-done(((bf16[3072,768]{1,0:T(8,128)(2,1)}), bf16[768,768]{1,0:T(8,128)(2,1)}) %reduce-scatter.23.cloned.1.call-update) | async-done | bytes 1179664 | tf_op jit(solution)/shard_map/reduce_scatter | solution.py:231
  635.1 39.3 %reduce-scatter.17.cloned.1.call-done = bf16[192,1920]{1,0:T(8,128)(2,1)} async-done(((bf16[768,1920]{1,0:T(8,128)(2,1)}), bf16[192,1920]{1,0:T(8,128)(2,1)}) %reduce-scatter.17.cloned.1.call-update) | async-done | bytes 737296 | tf_op jit(solution)/shard_map/reduce_scatter | solution.py:222
  674.4 9.3 %fusion.72 = bf16[1,512,768]{2,1,0:T(8,128)(2,1)} fusion(f32[512,768]{1,0:T(8,128)} %copy-done.9, bf16[3072,768]{1,0:T(8,128)(2,1)} %all-gather.19.cloned.1.call-done, f32[512,3072]{1,0:T(8,128)} %fusion.88), kind=kOutput, calls=%fused_computation.108 | convolution fusion | flops 2430861312 | bytes 13369344 | tf_op jit(solution)/shard_map/dot_general | solution.py:129
  689.3 7.8 reduce-scatter.25.cloned.1.call-done
  698.1 21.2 %reduce-scatter.27.cloned.1.call-done = bf16[192,2]{1,0:T(8,128)(2,1)} async-done(((bf16[768,2]{1,0:T(8,128)(2,1)}), bf16[192,2]{1,0:T(8,128)(2,1)}) %reduce-scatter.27.cloned.1.call-update) | async-done | bytes 784
  720.1 22.1 %all-reduce = (bf16[2,192]{1,0:T(2,128)(2,1)S(1)}, bf16[2,192]{1,0:T(2,128)(2,1)S(1)}) all-reduce(bf16[2,192]{1,0:T(2,128)(2,1)S(1)} %copy.92, bf16[2,192]{1,0:T(2,128)(2,1)S(1)} %copy.94), channel_id=1, replica_groups=mesh['dp'=2,'ctx'=4,'fsdp'=4] {'dp','ctx'}, use_global_device_ids=true, to_apply=%region_22.23 | all-reduce | flops 768 | bytes 3072 | tf_op jit(solution)/shard_map/psum | solution.py:236
  743.4 116.9 %all-reduce.4.cloned.1.call-done = (bf16[192,1920]{1,0:T(8,128)(2,1)}, bf16[192,768]{1,0:T(8,128)(2,1)}, bf16[768,768]{1,0:T(8,128)(2,1)}, bf16[768,768]{1,0:T(8,128)(2,1)}) async-done(((bf16[192,1920]{1,0:T(8,128)(2,1)}, bf16[192,768]{1,0:T(8,128)(2,1)}, bf16[768,768]{1,0:T(8,128)(2,1)}, bf16[768,768]{1,0:T(8,128)(2,1)}), (bf16[192,1920]{1,0:T(8,128)(2,1)}, bf16[192,768]{1,0:T(8,128)(2,1)}, ...) | async-done | bytes 3391504 | tf_op jit(solution)/shard_map/psum | solution.py:238
  (320 shorter events, 263.7 us)
Async XLA Ops:
  7.2 41.4 %copy-start = (s32[1,2048]{1,0:T(1,128)S(1)}, s32[1,2048]{1,0:T(1,128)}, u32[]{:S(2)}) copy-start(s32[1,2048]{1,0:T(1,128)} %param.19) | copy-start | bytes 24580
  7.2 32.5 %all-gather.9.cloned.1.call-start = ((), (), s32[]{:S(2)}) async-start(), calls=%async_computation.8 | async-start | bytes 3686400 | tf_op jit(solution)/shard_map/all_gather | solution.py:64
  7.9 100.7 %all-gather.13.cloned.1.call-start = ((), (), s32[]{:S(2)}) async-start(), calls=%async_computation.10 | async-start | bytes 3932160 | tf_op jit(solution)/shard_map/all_gather | solution.py:81
  20.0 19.8 %copy-start.24 = (f32[768]{0:T(1024)}, f32[768]{0:T(1024)S(1)}, u32[]{:S(2)}) copy-start(f32[768]{0:T(1024)S(1)} %get-tuple-element.570) | copy-start | bytes 9220
  45.0 128.0 %all-gather.11.cloned.1.call-start = ((), (), s32[]{:S(2)}) async-start(), calls=%async_computation.9 | async-start | bytes 3932160 | tf_op jit(solution)/shard_map/all_gather | solution.py:82
  46.1 166.2 %all-gather.15.cloned.1.call-start = ((), (), s32[]{:S(2)}) async-start(), calls=%async_computation.11 | async-start | bytes 1474560 | tf_op jit(solution)/shard_map/all_gather | solution.py:65
  46.7 182.8 %all-gather.17.cloned.1.call-start = ((), (), s32[]{:S(2)}) async-start(), calls=%async_computation.12 | async-start | bytes 5898240 | tf_op jit(solution)/shard_map/all_gather | solution.py:66
  47.3 221.1 %all-gather.19.cloned.1.call-start = ((), (), s32[]{:S(2)}) async-start(), calls=%async_computation.13 | async-start | bytes 5898240 | tf_op jit(solution)/shard_map/all_gather | solution.py:67
  47.8 394.9 %reduce-scatter.15.cloned.1.call-start = ((), (), s32[]{:S(2)}) async-start(), calls=%async_computation.15 | async-start | bytes 3932160 | tf_op jit(solution)/shard_map/reduce_scatter | solution.py:194
  188.3 24.0 %copy-start.7 = (bf16[1,512,768]{2,1,0:T(8,128)(2,1)S(1)}, bf16[1,512,768]{2,1,0:T(8,128)(2,1)}, u32[]{:S(2)}) copy-start(bf16[1,512,768]{2,1,0:T(8,128)(2,1)} %param.17) | copy-start | bytes 2359300
  229.5 38.9 %copy-start.13 = (bf16[1,512,768]{2,1,0:T(8,128)(2,1)S(1)}, bf16[1,512,768]{2,1,0:T(8,128)(2,1)}, u32[]{:S(2)}) copy-start(bf16[1,512,768]{2,1,0:T(8,128)(2,1)} %param.27) | copy-start | bytes 2359300
  382.3 123.0 %reduce-scatter.13.cloned.1.call-start = ((), (), s32[]{:S(2)}) async-start(), calls=%async_computation.14 | async-start | bytes 3932160 | tf_op jit(solution)/shard_map/reduce_scatter | solution.py:191
  391.3 143.0 %reduce-scatter.19.cloned.1.call-start = ((), (), s32[]{:S(2)}) async-start(), calls=%async_computation.17 | async-start | bytes 1474560 | tf_op jit(solution)/shard_map/reduce_scatter | solution.py:225
  394.4 190.2 %reduce-scatter.21.cloned.1.call-start = ((), (), s32[]{:S(2)}) async-start(), calls=%async_computation.18 | async-start | bytes 5898240 | tf_op jit(solution)/shard_map/reduce_scatter | solution.py:228
  401.0 234.0 %reduce-scatter.23.cloned.1.call-start = ((), (), s32[]{:S(2)}) async-start(), calls=%async_computation.19 | async-start | bytes 5898240 | tf_op jit(solution)/shard_map/reduce_scatter | solution.py:231
  410.4 94.9 %copy-start.8 = (bf16[1,512,768]{2,1,0:T(8,128)(2,1)S(1)}, bf16[1,512,768]{2,1,0:T(8,128)(2,1)}, u32[]{:S(2)}) copy-start(bf16[1,512,768]{2,1,0:T(8,128)(2,1)} %param.17) | copy-start | bytes 2359300
  410.5 94.9 %copy-start.25 = (f32[768]{0:T(1024)S(1)}, f32[768]{0:T(1024)}, u32[]{:S(2)}) copy-start(f32[768]{0:T(1024)} %copy-done.24) | copy-start | bytes 9220
  410.5 94.9 %copy-start.27 = (f32[512]{0:T(512)S(1)}, f32[512]{0:T(512)}, u32[]{:S(2)}) copy-start(f32[512]{0:T(512)} %copy-done.26) | copy-start | bytes 6148
  410.5 94.8 %copy-start.29 = (f32[512]{0:T(512)S(1)}, f32[512]{0:T(512)}, u32[]{:S(2)}) copy-start(f32[512]{0:T(512)} %copy-done.28) | copy-start | bytes 6148
  410.5 94.8 %copy-start.35 = (f32[768]{0:T(1024)S(1)}, f32[768]{0:T(1024)}, u32[]{:S(2)}) copy-start(f32[768]{0:T(1024)} %copy-done.34) | copy-start | bytes 9220
  410.5 263.9 %reduce-scatter.17.cloned.1.call-start = ((), (), s32[]{:S(2)}) async-start(), calls=%async_computation.16 | async-start | bytes 3686400 | tf_op jit(solution)/shard_map/reduce_scatter | solution.py:222
  510.5 186.6 %reduce-scatter.25.cloned.1.call-start = ((), (), s32[]{:S(2)}) async-start(), calls=%async_computation.20 | async-start | bytes 245760
  517.6 201.6 %reduce-scatter.27.cloned.1.call-start = ((), (), s32[]{:S(2)}) async-start(), calls=%async_computation.21 | async-start | bytes 245760
  518.6 341.7 %all-reduce.4.cloned.1.call-start = ((), (), s32[]{:S(2)}) async-start(), calls=%async_computation.22 | async-start | bytes 6782976 | tf_op jit(solution)/shard_map/psum | solution.py:238
  (43 other events, 182.5 us)
Sparse Core Ops, SparseCore 0:
  9.6 30.1 all-gather.8
  45.1 63.4 all-gather.12
  110.8 62.1 all-gather.10
  174.4 16.0 all-gather.14
  192.0 37.4 all-gather.16
  230.9 37.4 all-gather.18
  382.4 60.2 reduce-scatter.14
  445.0 60.2 reduce-scatter.12
  508.5 25.7 reduce-scatter.18
  536.8 47.8 reduce-scatter.20
  587.2 47.8 reduce-scatter.22
  637.6 36.7 reduce-scatter.16
  677.4 19.7 reduce-scatter.24
  699.5 19.7 reduce-scatter.26
  723.1 137.1 all-reduce.3
where the time goes:
time: 879 us; the launch traced here: 875 us
  waiting for transfers between devices  522 us (59%)
  matrix products  180 us (20%)
  local copies, waits for them, and re-layouts  80.6 us (9%)
  other arithmetic  41 us (5%)
  blocking collectives  33.8 us (4%)
  between operations  14.8 us (2%)
    psum x1, waiting for transfers between devices, body(): lax.psum(shares[2].astype(jnp.bfloat16), ('dp', 'ctx')).astype(jnp.float32)  117 us
    reduce_scatter x1, waiting for transfers between devices, body(): lax.psum_scatter(dkeys_all.astype(jnp.bfloat16), 'ctx', scatter_dimension...  60.4 us
    reduce_scatter x1, waiting for transfers between devices, body(): lax.psum_scatter(up_grad.astype(jnp.bfloat16), 'fsdp', scatter_dimension=...  50.4 us
    reduce_scatter x1, waiting for transfers between devices, body(): lax.psum_scatter(down_grad.astype(jnp.bfloat16), 'fsdp', scatter_dimensio...  50.4 us
    all_gather x1, waiting for transfers between devices, body(): lax.all_gather(key_low, 'ctx', axis=0, tiled=True)  43.7 us
    reduce_scatter x1, waiting for transfers between devices, body(): lax.psum_scatter(qkv_grad.astype(jnp.bfloat16), 'fsdp', scatter_dimension...  39.3 us
    unnamed x17, waiting for transfers between devices  31.5 us
    all_gather x1, waiting for transfers between devices, body(): lax.all_gather(w_down, 'fsdp', axis=0, tiled=True)  30.7 us
  transfers between devices with their start and end apart: 15, of which 14 were waited for; matrix products, arithmetic and copies ran while one was open for 19% of the time, Pallas kernels for 0%

commit v1 on v0

--- a/solution.py
+++ b/solution.py
@@ -9,6 +9,7 @@
 VH = 6
 EPSILON = 1e-05
 NEGATIVE = -1e30
+panel_proceed = lambda xx: jnp.sum(lax.all_gather(xx, axis_name=("dp", "ctx")), 0)
 
 
 def norm_layer(values_in, gain, bias):
@@ -233,7 +234,7 @@
         ).astype(jnp.float32),
     )
     summed = (
-        lax.psum(shares[0].astype(jnp.bfloat16), ("dp", "ctx")).astype(jnp.float32),
+        panel_proceed(shares[0].astype(jnp.bfloat16)).astype(jnp.float32),
         lax.psum(shares[1].astype(jnp.bfloat16), ("dp", "ctx")).astype(jnp.float32),
         lax.psum(shares[2].astype(jnp.bfloat16), ("dp", "ctx")).astype(jnp.float32),
         lax.psum(shares[3].astype(jnp.bfloat16), ("dp", "ctx")).astype(jnp.float32),

time: 879 us -> 879 us (level)
  blocking collectives: 33.8 us -> 54.4 us
  waiting for transfers between devices: 522 us -> 502 us
    unnamed x17, waiting for transfers between devices: 31.5 us -> 10.3 us
    all_gather x0 -> x1, blocking collectives: none -> 20.5 us  [lax.all_gather(xx, axis_name=('dp', 'ctx'))]
where the time goes in v1:
time: 879 us; the launch traced here: 874 us
  waiting for transfers between devices  502 us (57%)
  matrix products  180 us (20%)
  local copies, waits for them, and re-layouts  80.7 us (9%)
  blocking collectives  54.4 us (6%)
  other arithmetic  41 us (5%)
  between operations  14.8 us (2%)
    psum x1, waiting for transfers between devices, body(): lax.psum(shares[2].astype(jnp.bfloat16), ('dp', 'ctx')).astype(jnp.float32)  117 us
    reduce_scatter x1, waiting for transfers between devices, body(): lax.psum_scatter(dkeys_all.astype(jnp.bfloat16), 'ctx', scatter_dimension...  60.5 us
    reduce_scatter x1, waiting for transfers between devices, body(): lax.psum_scatter(up_grad.astype(jnp.bfloat16), 'fsdp', scatter_dimension=...  50.4 us
    reduce_scatter x1, waiting for transfers between devices, body(): lax.psum_scatter(down_grad.astype(jnp.bfloat16), 'fsdp', scatter_dimensio...  50.4 us
    all_gather x1, waiting for transfers between devices, body(): lax.all_gather(key_low, 'ctx', axis=0, tiled=True)  43.7 us
    reduce_scatter x1, waiting for transfers between devices, body(): lax.psum_scatter(qkv_grad.astype(jnp.bfloat16), 'fsdp', scatter_dimension...  39.3 us
    all_gather x1, waiting for transfers between devices, body(): lax.all_gather(w_down, 'fsdp', axis=0, tiled=True)  30.7 us
    reduce_scatter x1, waiting for transfers between devices, body(): lax.psum_scatter(dvalues_all.astype(jnp.bfloat16), 'ctx', scatter_dimensi...  29.8 us
  transfers between devices with their start and end apart: 15, of which 14 were waited for; matrix products, arithmetic and copies ran while one was open for 19% of the time, Pallas kernels for 0%

profile of v1, /device:TPU:0, one launch (start us, length us, event | category | flops | bytes accessed | tf_op | source)
XLA Modules:
  0.0 874.5 jit_solution(11011141911040499158)
XLA Ops:
  23.6 16.1 %all-gather.11.cloned.1.call-done = bf16[768,1920]{1,0:T(8,128)(2,1)} async-done(((bf16[192,1920]{1,0:T(8,128)(2,1)}), bf16[768,1920]{1,0:T(8,128)(2,1)}) %all-gather.11.cloned.1.call-update) | async-done | bytes 2949136 | tf_op jit(solution)/shard_map/all_gather | solution.py:65
  51.7 11.8 %gather_fusion = s32[2048]{0:T(1024)S(1)} fusion(s32[2048]{0:T(1024)S(1)} %bitcast.285, s32[2048]{0:T(1024)S(1)} %broadcast_clamp_fusion), kind=kCustom, calls=%fused_computation | custom fusion | bytes 24576 | tf_op jit(solution)/shard_map/jit(_take)/gather | solution.py:60
  65.0 43.7 %all-gather.15.cloned.1.call-done = bf16[2048,768]{1,0:T(8,128)(2,1)} async-done(((bf16[512,768]{1,0:T(8,128)(2,1)}), bf16[2048,768]{1,0:T(8,128)(2,1)}) %all-gather.15.cloned.1.call-update) | async-done | bytes 3145744 | tf_op jit(solution)/shard_map/all_gather | solution.py:82
  123.9 24.9 %while.39 = (s32[]{:T(128)}, f32[12,512]{1,0:T(8,128)S(1)}, f32[12,512]{1,0:T(8,128)S(1)}, s32[4,512]{1,0:T(4,128)S(1)}, s32[4,512]{1,0:T(4,128)S(1)}, /*index=5...) while((s32[]{:T(128)}, f32[12,512]{1,0:T(8,128)S(1)}, ...), condition=%wide.region_5.6_spmd.clone, body=%wide.region_2.5_spmd.clone.sunk | while | flops 425490944 | bytes 27867280 | solution.py:103
  148.8 24.2 %all-gather.13.cloned.1.call-done = bf16[2048,768]{1,0:T(8,128)(2,1)} async-done(((bf16[512,768]{1,0:T(8,128)(2,1)}), bf16[2048,768]{1,0:T(8,128)(2,1)}) %all-gather.13.cloned.1.call-update) | async-done | bytes 3145744 | tf_op jit(solution)/shard_map/all_gather | solution.py:83
  188.3 23.0 %while.40 = (s32[]{:T(128)}, f32[512,12,64]{0,2,1:T(8,128)S(1)}, bf16[4,512,12,64]{1,3,2,0:T(8,128)(2,1)}, s32[4,512]{1,0:T(4,128)S(1)}, s32[4,512]{1,0:T(4,128)...) while((s32[]{:T(128)}, f32[512,12,64]{0,2,1:T(8,128)S(1)}, ...), condition=%wide.region_7.8_spmd.clone, body=%wide.region_6.7_spmd.clone.sunk | while | flops 819462656 | bytes 6078098 | solution.py:118
  216.2 13.3 %all-gather.19.cloned.1.call-done = bf16[768,3072]{1,0:T(8,128)(2,1)} async-done(((bf16[768,768]{1,0:T(8,128)(2,1)}), bf16[768,3072]{1,0:T(8,128)(2,1)}) %all-gather.19.cloned.1.call-update) | async-done | bytes 4718608 | tf_op jit(solution)/shard_map/all_gather | solution.py:67
  229.5 8.2 fusion.88
  237.7 30.7 %all-gather.21.cloned.1.call-done = bf16[3072,768]{1,0:T(8,128)(2,1)} async-done(((bf16[768,768]{1,0:T(8,128)(2,1)}), bf16[3072,768]{1,0:T(8,128)(2,1)}) %all-gather.21.cloned.1.call-update) | async-done | bytes 4718608 | tf_op jit(solution)/shard_map/all_gather | solution.py:68
  268.4 9.3 %fusion.58 = bf16[512,3072]{1,0:T(8,128)(2,1)S(1)} fusion(f32[512,3072]{1,0:T(8,128)} %fusion.88, bf16[3072,768]{1,0:T(8,128)(2,1)} %all-gather.21.cloned.1.call-done, bf16[1,512,768]{2,1,0:T(8,128)(2,1)S(1)} %copy-done.13), kind=kOutput, calls=%fused_computation.72 | convolution fusion | flops 2447376384 | bytes 14942208 | tf_op jit(solution)/shard_map/dot_general | solution.py:148
  287.0 88.2 %while.41 = (s32[]{:T(128)}, f32[512,12,64]{0,2,1:T(8,128)}, f32[4,512,12,64]{1,3,2,0:T(8,128)}, bf16[4,512,12,64]{1,3,2,0:T(8,128)(2,1)}, bf16[4,512,12,64]{1,3...) while((s32[]{:T(128)}, f32[512,12,64]{0,2,1:T(8,128)}, ...), condition=%wide.region_14.15_spmd.clone, body=%wide.region_13.14_spmd.clone.sunk | while | flops 2046296576 | bytes 81885488 | solution.py:184
  394.5 6.5 convolution_convert_fusion.1
  402.1 8.3 convolution_convert_fusion
  412.9 29.8 %reduce-scatter.15.cloned.1.call-done = bf16[512,768]{0,1:T(8,128)(2,1)} async-done(((bf16[2048,768]{0,1:T(8,128)(2,1)}), bf16[512,768]{0,1:T(8,128)(2,1)}) %reduce-scatter.15.cloned.1.call-update) | async-done | bytes 786448 | tf_op jit(solution)/shard_map/reduce_scatter | solution.py:195
  444.8 60.5 %reduce-scatter.13.cloned.1.call-done = bf16[512,768]{0,1:T(8,128)(2,1)} async-done(((bf16[2048,768]{0,1:T(8,128)(2,1)}), bf16[512,768]{0,1:T(8,128)(2,1)}) %reduce-scatter.13.cloned.1.call-update) | async-done | bytes 786448 | tf_op jit(solution)/shard_map/reduce_scatter | solution.py:192
  518.8 15.4 %reduce-scatter.19.cloned.1.call-done = bf16[192,768]{1,0:T(8,128)(2,1)} async-done(((bf16[768,768]{1,0:T(8,128)(2,1)}), bf16[192,768]{1,0:T(8,128)(2,1)}) %reduce-scatter.19.cloned.1.call-update) | async-done | bytes 294928 | tf_op jit(solution)/shard_map/reduce_scatter | solution.py:226
  534.2 50.4 %reduce-scatter.21.cloned.1.call-done = bf16[768,768]{1,0:T(8,128)(2,1)} async-done(((bf16[768,3072]{1,0:T(8,128)(2,1)}), bf16[768,768]{1,0:T(8,128)(2,1)}) %reduce-scatter.21.cloned.1.call-update) | async-done | bytes 1179664 | tf_op jit(solution)/shard_map/reduce_scatter | solution.py:229
  584.6 50.4 %reduce-scatter.23.cloned.1.call-done = bf16[768,768]{1,0:T(8,128)(2,1)} async-done(((bf16[3072,768]{1,0:T(8,128)(2,1)}), bf16[768,768]{1,0:T(8,128)(2,1)}) %reduce-scatter.23.cloned.1.call-update) | async-done | bytes 1179664 | tf_op jit(solution)/shard_map/reduce_scatter | solution.py:232
  635.0 39.3 %reduce-scatter.17.cloned.1.call-done = bf16[192,1920]{1,0:T(8,128)(2,1)} async-done(((bf16[768,1920]{1,0:T(8,128)(2,1)}), bf16[192,1920]{1,0:T(8,128)(2,1)}) %reduce-scatter.17.cloned.1.call-update) | async-done | bytes 737296 | tf_op jit(solution)/shard_map/reduce_scatter | solution.py:223
  674.4 9.3 %fusion.72 = bf16[1,512,768]{2,1,0:T(8,128)(2,1)} fusion(f32[512,768]{1,0:T(8,128)} %copy-done.9, bf16[3072,768]{1,0:T(8,128)(2,1)} %all-gather.21.cloned.1.call-done, f32[512,3072]{1,0:T(8,128)} %fusion.88), kind=kOutput, calls=%fused_computation.108 | convolution fusion | flops 2430861312 | bytes 13369344 | tf_op jit(solution)/shard_map/dot_general | solution.py:130
  689.3 7.8 reduce-scatter.25.cloned.1.call-done
  698.0 20.5 %all-gather.3 = bf16[8,2,192]{2,1,0:T(2,128)(2,1)S(1)} all-gather(bf16[1,2,192]{2,1,0:T(2,128)(2,1)S(1)} %bitcast.323), channel_id=2, replica_groups=mesh['dp'=2,'ctx'=4,'fsdp'=4] {'dp','ctx'}, dimensions={0}, use_global_device_ids=true | all-gather | bytes 6912 | tf_op jit(solution)/shard_map/all_gather | solution.py:12
  720.1 22.1 %psum.35 = bf16[2,192]{1,0:T(2,128)(2,1)S(1)} all-reduce(bf16[2,192]{1,0:T(2,128)(2,1)S(1)} %copy.94), channel_id=1, replica_groups=mesh['dp'=2,'ctx'=4,'fsdp'=4] {'dp','ctx'}, use_global_device_ids=true, to_apply=%region_26.27 | all-reduce | flops 384 | bytes 1536 | tf_op jit(solution)/shard_map/psum | solution.py:238
  742.8 117.5 %all-reduce.3.cloned.1.call-done = (bf16[192,1920]{1,0:T(8,128)(2,1)}, bf16[192,768]{1,0:T(8,128)(2,1)}, bf16[768,768]{1,0:T(8,128)(2,1)}, bf16[768,768]{1,0:T(8,128)(2,1)}) async-done(((bf16[192,1920]{1,0:T(8,128)(2,1)}, bf16[192,768]{1,0:T(8,128)(2,1)}, bf16[768,768]{1,0:T(8,128)(2,1)}, bf16[768,768]{1,0:T(8,128)(2,1)}), (bf16[192,1920]{1,0:T(8,128)(2,1)}, bf16[192,768]{1,0:T(8,128)(2,1)}, ...) | async-done | bytes 3391504 | tf_op jit(solution)/shard_map/psum | solution.py:239
  (322 shorter events, 263.8 us)
Async XLA Ops:
  7.2 41.4 %copy-start = (s32[1,2048]{1,0:T(1,128)S(1)}, s32[1,2048]{1,0:T(1,128)}, u32[]{:S(2)}) copy-start(s32[1,2048]{1,0:T(1,128)} %param.19) | copy-start | bytes 24580
  7.2 32.5 %all-gather.11.cloned.1.call-start = ((), (), s32[]{:S(2)}) async-start(), calls=%async_computation.8 | async-start | bytes 3686400 | tf_op jit(solution)/shard_map/all_gather | solution.py:65
  7.9 100.7 %all-gather.15.cloned.1.call-start = ((), (), s32[]{:S(2)}) async-start(), calls=%async_computation.10 | async-start | bytes 3932160 | tf_op jit(solution)/shard_map/all_gather | solution.py:82
  20.0 19.8 %copy-start.24 = (f32[768]{0:T(1024)}, f32[768]{0:T(1024)S(1)}, u32[]{:S(2)}) copy-start(f32[768]{0:T(1024)S(1)} %get-tuple-element.568) | copy-start | bytes 9220
  45.0 128.0 %all-gather.13.cloned.1.call-start = ((), (), s32[]{:S(2)}) async-start(), calls=%async_computation.9 | async-start | bytes 3932160 | tf_op jit(solution)/shard_map/all_gather | solution.py:83
  46.1 166.2 %all-gather.17.cloned.1.call-start = ((), (), s32[]{:S(2)}) async-start(), calls=%async_computation.11 | async-start | bytes 1474560 | tf_op jit(solution)/shard_map/all_gather | solution.py:66
  46.7 182.8 %all-gather.19.cloned.1.call-start = ((), (), s32[]{:S(2)}) async-start(), calls=%async_computation.12 | async-start | bytes 5898240 | tf_op jit(solution)/shard_map/all_gather | solution.py:67
  47.3 221.2 %all-gather.21.cloned.1.call-start = ((), (), s32[]{:S(2)}) async-start(), calls=%async_computation.13 | async-start | bytes 5898240 | tf_op jit(solution)/shard_map/all_gather | solution.py:68
  47.8 394.8 %reduce-scatter.15.cloned.1.call-start = ((), (), s32[]{:S(2)}) async-start(), calls=%async_computation.15 | async-start | bytes 3932160 | tf_op jit(solution)/shard_map/reduce_scatter | solution.py:195
  188.3 24.0 %copy-start.7 = (bf16[1,512,768]{2,1,0:T(8,128)(2,1)S(1)}, bf16[1,512,768]{2,1,0:T(8,128)(2,1)}, u32[]{:S(2)}) copy-start(bf16[1,512,768]{2,1,0:T(8,128)(2,1)} %param.17) | copy-start | bytes 2359300
  229.5 38.9 %copy-start.13 = (bf16[1,512,768]{2,1,0:T(8,128)(2,1)S(1)}, bf16[1,512,768]{2,1,0:T(8,128)(2,1)}, u32[]{:S(2)}) copy-start(bf16[1,512,768]{2,1,0:T(8,128)(2,1)} %param.27) | copy-start | bytes 2359300
  382.3 123.0 %reduce-scatter.13.cloned.1.call-start = ((), (), s32[]{:S(2)}) async-start(), calls=%async_computation.14 | async-start | bytes 3932160 | tf_op jit(solution)/shard_map/reduce_scatter | solution.py:192
  391.3 143.0 %reduce-scatter.19.cloned.1.call-start = ((), (), s32[]{:S(2)}) async-start(), calls=%async_computation.17 | async-start | bytes 1474560 | tf_op jit(solution)/shard_map/reduce_scatter | solution.py:226
  394.4 190.2 %reduce-scatter.21.cloned.1.call-start = ((), (), s32[]{:S(2)}) async-start(), calls=%async_computation.18 | async-start | bytes 5898240 | tf_op jit(solution)/shard_map/reduce_scatter | solution.py:229
  401.0 234.0 %reduce-scatter.23.cloned.1.call-start = ((), (), s32[]{:S(2)}) async-start(), calls=%async_computation.19 | async-start | bytes 5898240 | tf_op jit(solution)/shard_map/reduce_scatter | solution.py:232
  410.4 94.9 %copy-start.8 = (bf16[1,512,768]{2,1,0:T(8,128)(2,1)S(1)}, bf16[1,512,768]{2,1,0:T(8,128)(2,1)}, u32[]{:S(2)}) copy-start(bf16[1,512,768]{2,1,0:T(8,128)(2,1)} %param.17) | copy-start | bytes 2359300
  410.4 94.9 %copy-start.25 = (f32[768]{0:T(1024)S(1)}, f32[768]{0:T(1024)}, u32[]{:S(2)}) copy-start(f32[768]{0:T(1024)} %copy-done.24) | copy-start | bytes 9220
  410.4 94.9 %copy-start.27 = (f32[512]{0:T(512)S(1)}, f32[512]{0:T(512)}, u32[]{:S(2)}) copy-start(f32[512]{0:T(512)} %copy-done.26) | copy-start | bytes 6148
  410.5 94.8 %copy-start.29 = (f32[512]{0:T(512)S(1)}, f32[512]{0:T(512)}, u32[]{:S(2)}) copy-start(f32[512]{0:T(512)} %copy-done.28) | copy-start | bytes 6148
  410.5 94.8 %copy-start.35 = (f32[768]{0:T(1024)S(1)}, f32[768]{0:T(1024)}, u32[]{:S(2)}) copy-start(f32[768]{0:T(1024)} %copy-done.34) | copy-start | bytes 9220
  410.5 263.9 %reduce-scatter.17.cloned.1.call-start = ((), (), s32[]{:S(2)}) async-start(), calls=%async_computation.16 | async-start | bytes 3686400 | tf_op jit(solution)/shard_map/reduce_scatter | solution.py:223
  510.5 186.6 %reduce-scatter.25.cloned.1.call-start = ((), (), s32[]{:S(2)}) async-start(), calls=%async_computation.20 | async-start | bytes 245760
  517.6 201.6 %reduce-scatter.27.cloned.1.call-start = ((), (), s32[]{:S(2)}) async-start(), calls=%async_computation.21 | async-start | bytes 245760
  518.5 341.7 %all-reduce.3.cloned.1.call-start = ((), (), s32[]{:S(2)}) async-start(), calls=%async_computation.22 | async-start | bytes 6782976 | tf_op jit(solution)/shard_map/psum | solution.py:239
  (43 other events, 182.5 us)
Sparse Core Ops, SparseCore 0:
  9.6 30.1 all-gather.10
  45.1 63.4 all-gather.14
  110.8 62.1 all-gather.12
  174.4 16.0 all-gather.16
  192.0 37.4 all-gather.18
  230.9 37.4 all-gather.20
  382.4 60.2 reduce-scatter.14
  445.0 60.2 reduce-scatter.12
  508.4 25.7 reduce-scatter.18
  536.8 47.8 reduce-scatter.20
  587.2 47.8 reduce-scatter.22
  637.6 36.7 reduce-scatter.16
  677.4 19.7 reduce-scatter.24
  699.5 19.7 reduce-scatter.26
  723.1 137.1 all-reduce.2
